TPU v7x, 32 devices: a whole 2x2x4 slice. The times are simulated.
32 devices in a mesh: grp: 4 (over x, core), dev: 8 (over z, y).
Axes of the slice: x: 2, y: 2, z: 4, core: 2. Of those that a mesh axis runs over, the one named last changes fastest.
Arguments:
- coefficients: float32 [2, 8, 64, 4096], P(None, None, None, ('grp', 'dev')), may hold values from -6 to 6
- spatial_root: int32 [64], replicated, may hold values from 0 to 1023
- frequency_root: int32 [64], replicated, may hold values from 0 to 255
Outputs:
- result: float32 [2, 8, 64, 4096], P(None, None, None, ('grp', 'dev'))
All inputs are finite; a program needn't handle non-finite values.
Results may differ from a plain program's by a relative error of at most 0.002.
Values sent between devices are 32-bit elements; how exact they have to be, the bound alone decides.
A program may use at most 64 MiB of HBM per device.

v0:
```python
import math

import jax
import jax.numpy as jnp
from jax import lax
from jax.sharding import PartitionSpec as P

LEVELS = 12


HIGHEST = lax.Precision.HIGHEST


def partner_2(block, axis, distance):
    count = lax.axis_size(axis)
    route = []
    for low in range(count):
        high = low | 1 << distance
        if high != low and high < count:
            route += [(low, high), (high, low)]
    return lax.ppermute(block, axis, route)


def cheb_nodes():
    node_order = jnp.arange(8, dtype=jnp.float32)
    return 0.5 - 0.5 * jnp.cos(math.pi * (2.0 * node_order + 1.0) / 16.0)


def lagrange_table(half_cell):
    points = cheb_nodes()
    target = (points + half_cell) / 2.0
    diagonal = jnp.arange(8)[:, None] == jnp.arange(8)[None, :]
    numerator = jnp.where(
        diagonal[None, :, :], jnp.float32(1.0), target[:, None, None] - points[None, None, :]
    )
    denominator = jnp.where(diagonal, jnp.float32(1.0), points[:, None] - points[None, :])
    return jnp.prod(numerator, axis=2) / jnp.prod(denominator, axis=1)[None, :]


def interp_tables():
    halves = [lagrange_table(0.0), lagrange_table(1.0)]
    return jnp.stack(
        [jnp.kron(halves[quadrant % 2], halves[quadrant // 2]) for quadrant in range(4)]
    )


def pair_digits(pair_index, pairs_dev, devices_dev):
    quarter = pairs_dev // 4
    within = pair_index % pairs_dev
    device = pair_index // pairs_dev % devices_dev
    group_id = pair_index // (pairs_dev * devices_dev)
    places = [device % 4, group_id % 4, within // quarter]
    return (places, device // 4 * quarter + within % quarter)


def pair_boxes(pair_index, level_step, box_roots, pairs_dev, devices_dev, levels):
    places, _ = pair_digits(pair_index, pairs_dev, devices_dev)
    coarse_space = levels // 2 - 1
    coarse_wave = levels // 2 - 2
    space_row = box_roots[0] // 2**coarse_space
    space_column = box_roots[0] % 2**coarse_space
    for position in range(level_step):
        space_row = 2 * space_row + places[position] % 2
        space_column = 2 * space_column + places[position] // 2
    wave_row = box_roots[1] // 2**coarse_wave
    wave_column = box_roots[1] % 2**coarse_wave
    for position in range(2, level_step - 1, -1):
        wave_row = 2 * wave_row + places[position] % 2
        wave_column = 2 * wave_column + places[position] // 2
    space_side = 0.5 ** (coarse_space + level_step)
    wave_side = float(2**levels) / float(2 ** (coarse_wave + 3 - level_step))
    offset = -0.5 * float(2**levels)
    space_box = (
        space_row.astype(jnp.float32) * space_side,
        space_column.astype(jnp.float32) * space_side,
        space_side,
    )
    wave_box = (
        offset + wave_row.astype(jnp.float32) * wave_side,
        offset + wave_column.astype(jnp.float32) * wave_side,
        wave_side,
    )
    return (space_box, wave_box)


def box_points(square):
    points = cheb_nodes()
    first_axis = jnp.repeat(points, 8)
    second_axis = jnp.tile(points, 8)
    return (
        square[0][None, :] + square[2] * first_axis[:, None],
        square[1][None, :] + square[2] * second_axis[:, None],
    )


def box_center(square):
    return (square[0] + 0.5 * square[2], square[1] + 0.5 * square[2])


def phase_angle(first_space, second_space, first_wave, second_wave):
    two_pi = 2.0 * math.pi
    wave_speed = 16.0 * math.pi
    speed_one = (
        2.0 + jnp.sin(wave_speed * first_space) * jnp.sin(wave_speed * second_space)
    ) / 16.0
    speed_two = (
        2.0 + jnp.cos(wave_speed * first_space) * jnp.cos(wave_speed * second_space)
    ) / 16.0
    radial = jnp.sqrt(
        speed_one * speed_one * first_wave * first_wave
        + speed_two * speed_two * second_wave * second_wave
    )
    return two_pi * (first_space * first_wave + second_space * second_wave + radial)


def rotate(values, turn_angle):
    cosine = jnp.cos(turn_angle)
    sine_part = jnp.sin(turn_angle)
    return jnp.stack(
        [values[0] * cosine - values[1] * sine_part, values[0] * sine_part + values[1] * cosine]
    )


def pre_merge(
    children, new_index, new_roots, child_index, child_roots, pairs_dev, devices_dev, levels
):
    space_box, wave_box = pair_boxes(new_index, 1, new_roots, pairs_dev, devices_dev, levels)
    center_one, center_two = box_center(space_box)
    turned = []
    for child_id in range(4):
        _, child_wave = pair_boxes(
            child_index[child_id],
            0,
            (child_roots[0][child_id], child_roots[1][child_id]),
            pairs_dev,
            devices_dev,
            levels,
        )
        wave_one, wave_two = box_points(child_wave)
        turned.append(
            rotate(
                children[child_id],
                -phase_angle(center_one[None, :], center_two[None, :], wave_one, wave_two),
            )
        )
    summed = jnp.einsum("cst,caksm->aktm", interp_tables(), jnp.stack(turned), precision=HIGHEST)
    wave_one, wave_two = box_points(wave_box)
    return rotate(summed, phase_angle(center_one[None, :], center_two[None, :], wave_one, wave_two))


def switch_step(values, pair_index, box_roots, pairs_dev, devices_dev, levels):
    space_box, wave_box = pair_boxes(pair_index, 1, box_roots, pairs_dev, devices_dev, levels)
    space_one, space_two = box_points(space_box)
    wave_one, wave_two = box_points(wave_box)
    kernel_angle = phase_angle(
        space_one[:, None, :], space_two[:, None, :], wave_one[None, :, :], wave_two[None, :, :]
    )
    cosine = jnp.cos(kernel_angle)
    sine_part = jnp.sin(kernel_angle)
    real_part = jnp.einsum("tsm,ksm->ktm", cosine, values[0], precision=HIGHEST) - jnp.einsum(
        "tsm,ksm->ktm", sine_part, values[1], precision=HIGHEST
    )
    imag_part = jnp.einsum("tsm,ksm->ktm", sine_part, values[0], precision=HIGHEST) + jnp.einsum(
        "tsm,ksm->ktm", cosine, values[1], precision=HIGHEST
    )
    return jnp.stack([real_part, imag_part]) / 64.0


def post_terms(values, pair_index, box_roots, level_step, pairs_dev, devices_dev, levels):
    space_box, wave_box = pair_boxes(
        pair_index, level_step, box_roots, pairs_dev, devices_dev, levels
    )
    space_one, space_two = box_points(space_box)
    center_one, center_two = box_center(wave_box)
    return rotate(
        values, -phase_angle(space_one, space_two, center_one[None, :], center_two[None, :])
    )


def post_finish(merged, pair_index, box_roots, level_step, pairs_dev, devices_dev, levels):
    space_box, wave_box = pair_boxes(
        pair_index, level_step, box_roots, pairs_dev, devices_dev, levels
    )
    space_one, space_two = box_points(space_box)
    center_one, center_two = box_center(wave_box)
    return rotate(
        merged, phase_angle(space_one, space_two, center_one[None, :], center_two[None, :])
    )


def lookup_roots(pair_index, spatial_root, frequency_root, pairs_dev, devices_dev):
    _, block_id = pair_digits(pair_index, pairs_dev, devices_dev)
    matches = block_id[..., None] == jnp.arange(spatial_root.shape[0], dtype=jnp.int32)
    return (
        jnp.sum(jnp.where(matches, spatial_root, 0), axis=-1),
        jnp.sum(jnp.where(matches, frequency_root, 0), axis=-1),
    )


def middle_levels(first_level, held_index, held_roots, group_id, pairs_dev, devices_dev, total_fn):
    switched = switch_step(first_level, held_index, held_roots, pairs_dev, devices_dev, LEVELS)
    child_terms = post_terms(switched, held_index, held_roots, 1, pairs_dev, devices_dev, LEVELS)
    summed = total_fn(child_terms)
    local_interp = lax.dynamic_index_in_dim(interp_tables(), group_id, 0, keepdims=False)
    spread_level = jnp.einsum("ts,aksm->aktm", local_interp, summed, precision=HIGHEST)
    return post_finish(spread_level, held_index, held_roots, 2, pairs_dev, devices_dev, LEVELS)


def per_device(coefficients, spatial_root, frequency_root):
    rhs_count = coefficients.shape[1]
    rank_count = coefficients.shape[2]
    pairs_dev = coefficients.shape[3]
    devices_dev = lax.axis_size("dev")
    group_id = lax.axis_index("grp")
    device_id = lax.axis_index("dev")
    base_index = group_id * (devices_dev * pairs_dev)
    own_index = base_index + device_id * pairs_dev + jnp.arange(pairs_dev, dtype=jnp.int32)
    own_roots = lookup_roots(own_index, spatial_root, frequency_root, pairs_dev, devices_dev)
    stacked = coefficients[None]
    for bit_number in range(2):
        partner = partner_2(stacked, "dev", bit_number)
        upper_half = device_id // 2**bit_number % 2
        stacked = jnp.where(
            upper_half == 1,
            jnp.concatenate([partner, stacked]),
            jnp.concatenate([stacked, partner]),
        )
    child_index = (
        own_index[None, :] + (jnp.arange(4, dtype=jnp.int32)[:, None] - device_id % 4) * pairs_dev
    )
    child_roots = lookup_roots(child_index, spatial_root, frequency_root, pairs_dev, devices_dev)
    first_level = pre_merge(
        stacked, own_index, own_roots, child_index, child_roots, pairs_dev, devices_dev, LEVELS
    )
    second = middle_levels(
        first_level,
        own_index,
        own_roots,
        group_id,
        pairs_dev,
        devices_dev,
        lambda terms: lax.psum(terms, "grp"),
    )
    child_terms = post_terms(second, own_index, own_roots, 2, pairs_dev, devices_dev, LEVELS)
    summed = jnp.sum(child_terms.reshape(2, rhs_count, rank_count, 4, pairs_dev // 4), axis=3)
    spread_last = jnp.einsum("jts,aksm->aktjm", interp_tables(), summed, precision=HIGHEST).reshape(
        2, rhs_count, rank_count, pairs_dev
    )
    return post_finish(spread_last, own_index, own_roots, 3, pairs_dev, devices_dev, LEVELS)


def solution(mesh):
    return jax.shard_map(
        per_device,
        mesh=mesh,
        in_specs=(P(None, None, None, ("grp", "dev")), P(), P()),
        out_specs=P(None, None, None, ("grp", "dev")),
        check_vma=False,
    )
```

profile of v0, /device:TPU:0, one launch (start us, length us, event | category | flops | bytes accessed | tf_op | source)
XLA Modules:
  0.0 217.6 jit_solution(8685077930100766251)
XLA Ops:
  6.5 3.0 %collective-permute-start = (f32[1,2,8,64,128]{4,3,2,1,0:T(8,128)}, f32[1,2,8,64,128]{4,3,2,1,0:T(8,128)S(1)}, u32[]{:S(2)}, u32[]{:S(2)}) collective-permute-start(f32[1,2,8,64,128]{4,3,2,1,0:T(8,128)} %bitcast.157), channel_id=1, source_target_pairs={{0,1},{1,0},{2,3},{3,2},{4,5},{5,4},{6,7},{7,6},{8,9},{9,8},{10,11... | collective-permute-start | bytes 1572872 | tf_op jit(solution)/shard_map/ppermute | solution.py:21
  9.8 0.8 select_reduce_fusion.4
  10.8 0.8 select_reduce_fusion
  11.8 0.3 select_reduce_fusion.2
  12.8 0.5 fusion.152
  13.4 8.3 %collective-permute-done = f32[1,2,8,64,128]{4,3,2,1,0:T(8,128)S(1)} collective-permute-done((f32[1,2,8,64,128]{4,3,2,1,0:T(8,128)}, f32[1,2,8,64,128]{4,3,2,1,0:T(8,128)S(1)}, u32[]{:S(2)}, u32[]{:S(2)}) %collective-permute-start) | collective-permute-done | bytes 524320 | tf_op jit(solution)/shard_map/ppermute | solution.py:21
  21.7 1.4 maximum_select_fusion.1
  23.1 1.9 collective-permute-start.1
  26.2 0.8 fusion.150
  28.0 0.5 fusion.140
  28.4 19.0 %collective-permute-done.1 = f32[2,2,8,64,128]{4,3,2,1,0:T(8,128)S(1)} collective-permute-done((f32[2,2,8,64,128]{4,3,2,1,0:T(8,128)S(1)}, f32[2,2,8,64,128]{4,3,2,1,0:T(8,128)S(1)}, u32[]{:S(2)}, u32[]{:S(2)}) %collective-permute-start.1) | collective-permute-done | bytes 1048608 | tf_op jit(solution)/shard_map/ppermute | solution.py:21
  47.5 0.3 maximum_select_fusion
  48.3 1.5 fusion.46
  50.1 0.2 copy.62
  50.3 29.0 %fusion.2 = f32[128,8,64]{2,1,0:T(8,128)S(1)} fusion(f32[8,64,128]{1,0,2:T(8,128)S(1)} %copy.63, f32[64,128]{0,1:T(8,128)S(1)} %copy.61, f32[64,128]{0,1:T(8,128)S(1)} %copy.60, f32[64,128]{0,1:T(8,128)S(1)} %copy.59, f32[64,128]{0,1:T(8,128)S(1)} %copy.58, f32[64,128]{0,1:T(8,128)S(1)} %copy.57, f32[64,128]{0,1:T(8,128)S(1)} %copy.56), kind=kOutput, calls=%fused_computation.3 | convolution fusion | flops 55574528 | bytes 720896 | tf_op jit(solution)/shard_map/tsm,ksm->ktm/dot_general | solution.py:163
  79.3 28.8 %fusion.4 = f32[128,8,64]{2,1,0:T(8,128)S(1)} fusion(f32[8,64,128]{1,0,2:T(8,128)S(1)} %copy.62, f32[64,128]{0,1:T(8,128)S(1)} %copy.61, f32[64,128]{0,1:T(8,128)S(1)} %copy.60, f32[64,128]{0,1:T(8,128)S(1)} %copy.59, f32[64,128]{0,1:T(8,128)S(1)} %copy.58, f32[64,128]{0,1:T(8,128)S(1)} %copy.57, f32[64,128]{0,1:T(8,128)S(1)} %copy.56), kind=kOutput, calls=%fused_computation.4 | convolution fusion | flops 55574528 | bytes 720896 | tf_op jit(solution)/shard_map/tsm,ksm->ktm/dot_general | solution.py:160
  108.1 29.0 %fusion.58 = f32[1,8,64,128]{2,1,3,0:T(8,128)S(1)} fusion(f32[128,8,64]{2,1,0:T(8,128)S(1)} %fusion.2, f32[8,64,128]{1,0,2:T(8,128)S(1)} %copy.62, f32[64,128]{0,1:T(8,128)S(1)} %copy.61, f32[64,128]{0,1:T(8,128)S(1)} %copy.60, f32[64,128]{0,1:T(8,128)S(1)} %copy.59, f32[64,128]{0,1:T(8,128)S(1)} %copy.58, f32[64,128]{0,1:T(8,128)S(1)} %copy.57, ...), kind=kOutput, calls=%fused_computation.50 | convolution fusion | flops 55640064 | bytes 983040 | tf_op jit(solution)/shard_map/tsm,ksm->ktm/dot_general | solution.py:163
  137.1 29.0 %fusion.52 = f32[1,8,64,128]{2,1,3,0:T(8,128)S(1)} fusion(f32[128,8,64]{2,1,0:T(8,128)S(1)} %fusion.4, f32[8,64,128]{1,0,2:T(8,128)S(1)} %copy.63, f32[64,128]{0,1:T(8,128)S(1)} %copy.61, f32[64,128]{0,1:T(8,128)S(1)} %copy.60, f32[64,128]{0,1:T(8,128)S(1)} %copy.59, f32[64,128]{0,1:T(8,128)S(1)} %copy.58, f32[64,128]{0,1:T(8,128)S(1)} %copy.57, ...), kind=kOutput, calls=%fused_computation.48 | convolution fusion | flops 55640064 | bytes 983040 | tf_op jit(solution)/shard_map/tsm,ksm->ktm/dot_general | solution.py:160
  166.3 1.1 pad_maximum_fusion
  167.7 0.6 fusion.138
  168.3 36.7 %all-reduce.2.cloned.1.call-done = f32[2,8,64,128]{2,1,3,0:T(8,128)} async-done(((f32[2,8,64,128]{2,1,3,0:T(8,128)}), f32[2,8,64,128]{2,1,3,0:T(8,128)}) %all-reduce.2.cloned.1.call-update) | async-done | bytes 524304 | tf_op jit(solution)/shard_map/psum | solution.py:242
  205.1 2.6 %convolution_bitcast_fusion.1 = f32[2,8,64,128]{3,2,1,0:T(8,128)S(1)} fusion(f32[2,8,64,128]{2,1,3,0:T(8,128)} %all-reduce.2.cloned.1.call-done, f32[4,64,64]{1,2,0:T(8,128)S(1)} %constant_dynamic-update-slice_fusion, s32[]{:T(128)S(6)} %select_n.1084), kind=kOutput, calls=%fused_computation.46 | convolution fusion | flops 100663296 | bytes 1081348 | tf_op jit(solution)/shard_map/ts,aksm->aktm/dot_general | solution.py:205
  208.3 1.0 convolution_bitcast_fusion
  209.9 0.8 pad_maximum_fusion.1
  (82 shorter events, 5.9 us)
Async XLA Ops:
  6.5 198.5 %all-reduce.2.cloned.1.call-start = ((), (), s32[]{:S(2)}) async-start(), calls=%async_computation | async-start | bytes 2097152 | tf_op jit(solution)/shard_map/psum | solution.py:242
  6.5 15.1 %collective-permute-start = (f32[1,2,8,64,128]{4,3,2,1,0:T(8,128)}, f32[1,2,8,64,128]{4,3,2,1,0:T(8,128)S(1)}, u32[]{:S(2)}, u32[]{:S(2)}) collective-permute-start(f32[1,2,8,64,128]{4,3,2,1,0:T(8,128)} %bitcast.157), channel_id=1, source_target_pairs={{0,1},{1,0},{2,3},{3,2},{4,5},{5,4},{6,7},{7,6},{8,9},{9,8},{10,11... | collective-permute-start | bytes 1572872 | tf_op jit(solution)/shard_map/ppermute | solution.py:21
  23.1 24.4 %collective-permute-start.1 = (f32[2,2,8,64,128]{4,3,2,1,0:T(8,128)S(1)}, f32[2,2,8,64,128]{4,3,2,1,0:T(8,128)S(1)}, u32[]{:S(2)}, u32[]{:S(2)}) collective-permute-start(f32[2,2,8,64,128]{4,3,2,1,0:T(8,128)S(1)} %maximum_select_fusion.1), channel_id=1, source_target_pairs={{0,2},{2,0},{1,3},{3,1},{4,6},{6,4},{5,7},{7,5},{8,10},{10,8},{9,1... | collective-permute-start | bytes 3145736 | tf_op jit(solution)/shard_map/ppermute | solution.py:21
Sparse Core Ops, SparseCore 0:
  167.6 37.4 all-reduce.1
where the time goes:
time: 218 us
  matrix products  121 us (56%)
  waiting for transfers between devices  64 us (29%)
  between operations  14 us (6%)
  other arithmetic  10 us (5%)
  starting transfers between devices  4.86 us (2%)
  local copies, waits for them, and re-layouts  3.9 us (2%)
    psum x1, waiting for transfers between devices, per_device(): lax.psum(terms, 'grp')  36.7 us
    dot_general x1, matrix products, switch_step(): jnp.einsum('tsm,ksm->ktm', cosine, values[1], precision=HIGHEST)  29 us
    dot_general x1, matrix products, switch_step(): jnp.einsum('tsm,ksm->ktm', sine_part, values[0], precision=HIGHEST)  29 us
    dot_general x1, matrix products, switch_step(): jnp.einsum('tsm,ksm->ktm', sine_part, values[1], precision=HIGHEST)  29 us
    dot_general x1, matrix products, switch_step(): jnp.einsum('tsm,ksm->ktm', cosine, values[0], precision=HIGHEST)  28.8 us
    ppermute x2, waiting for transfers between devices, partner_2(): return lax.ppermute(block, axis, route)  27.3 us
    ppermute x2, starting transfers between devices, partner_2(): return lax.ppermute(block, axis, route)  4.86 us
  transfers between devices with their start and end apart: 3, of which 3 were waited for; matrix products, arithmetic and copies ran while one was open for 4% of the time, Pallas kernels for 0%

commit v1 on v0

v1 whole, which is shorter than its diff:
```python
import functools
import math

import jax
import jax.numpy as jnp
import ml_dtypes
import numpy as np
from jax import lax
from jax.experimental import pallas as pl
from jax.experimental.pallas import tpu as pltpu
from jax.sharding import PartitionSpec as P

LEVELS = 12
MESH = pl.DeviceIdType.MESH
LANES = 128
K_STEPS = 4
LAG_C = 3
LAG_E = 5

NODES = 0.5 - 0.5 * np.cos(np.pi * (2.0 * np.arange(8) + 1.0) / 16.0)


def lagrange(half):
    target = (NODES + half) / 2.0
    table = np.ones((8, 8))
    for s in range(8):
        for n in range(8):
            if n != s:
                table[:, s] *= (target - NODES[n]) / (NODES[s] - NODES[n])
    return table


HALVES = [lagrange(0.0), lagrange(1.0)]
INTERP = [np.kron(HALVES[u % 2], HALVES[u // 2]) for u in range(4)]


def split_table(matrix):
    wide = np.concatenate([matrix, matrix], axis=1)
    high = wide.astype(ml_dtypes.bfloat16)
    low = (wide - high.astype(np.float64)).astype(ml_dtypes.bfloat16)
    return np.concatenate([high, low], axis=0)


PRE_TABLE = np.stack(
    [split_table(np.concatenate([INTERP[u].T, INTERP[u ^ 1].T], axis=1)) for u in range(4)]
)
LAST_TABLE = np.stack(
    [split_table(np.concatenate([INTERP[j] @ INTERP[u] for j in range(4)], axis=1)) for u in range(4)]
)


def fit(function, degree):
    series = np.polynomial.chebyshev.Chebyshev.interpolate(function, degree, domain=[0.0, 0.2504])
    return series.convert(kind=np.polynomial.Polynomial, domain=[-1, 1], window=[-1, 1]).coef


def sine_over(g):
    f = np.sqrt(np.maximum(g, 1e-30))
    return np.sin(2 * np.pi * f) / f


COS_COEF = fit(lambda g: np.cos(2 * np.pi * np.sqrt(np.maximum(g, 0.0))), 6)
SIN_COEF = fit(sine_over, 6)


def horner(coef, g, scale):
    total = jnp.float32(coef[-1] * scale)
    for value in coef[-2::-1]:
        total = total * g + jnp.float32(value * scale)
    return total


def frac(turns):
    return turns - jnp.floor(turns + 0.5)


def cos_sin(turns, scale=1.0):
    f = frac(turns)
    g = f * f
    return horner(COS_COEF, g, scale), horner(SIN_COEF, g, scale) * f


def root_of(square):
    inverse = lax.rsqrt(square)
    first = square * inverse
    return first + (0.5 * inverse) * (square - first * first)


def speeds(x1, x2):
    cos1, sin1 = cos_sin(8.0 * x1)
    cos2, sin2 = cos_sin(8.0 * x2)
    one = (2.0 + sin1 * sin2) / 16.0
    two = (2.0 + cos1 * cos2) / 16.0
    return one * one, two * two


def turns_of(x1, x2, sq1, sq2, k1, k2):
    return (x1 * k1 + x2 * k2) + root_of(sq1 * (k1 * k1) + sq2 * (k2 * k2))


def flip(value, bit):
    return value + bit - 2 * bit * (value // bit % 2)


def split(values):
    high = values.astype(jnp.bfloat16)
    low = (values - high.astype(jnp.float32)).astype(jnp.bfloat16)
    return high, low


def kernel(
    space_ref, wave_ref, coef_hbm, pre_hbm, last_hbm, out_ref,
    own, from_y, to_z, from_z, part, packed, gathered,
    pre_tab, last_tab, rot_c, rot_s, ker_c, ker_s, pre_turn, fin_c, fin_s, spread,
    x_rows, x2k2, k_rows, rhs_pre, rhs_last,
    load_sem, ysend, yrecv, zsend, zrecv, gsend, grecv,
):
    rhs = coef_hbm.shape[1]
    grp = lax.axis_index("grp")
    dev = lax.axis_index("dev")
    u0 = dev % 4
    height = dev // 4
    dev_y = flip(dev, 1)
    dev_z = flip(dev, 2)
    peers = [flip(grp, 1), flip(grp, 2), flip(flip(grp, 1), 2)]

    barrier = pltpu.get_barrier_semaphore()
    for target in [(grp, dev_y), (grp, dev_z)] + [(peer, dev) for peer in peers]:
        pl.semaphore_signal(barrier, inc=1, device_id=target, device_id_type=MESH)
    loads = [
        pltpu.make_async_copy(coef_hbm, own, load_sem.at[0]),
        pltpu.make_async_copy(pre_hbm.at[u0], pre_tab, load_sem.at[1]),
        pltpu.make_async_copy(last_hbm.at[grp], last_tab, load_sem.at[2]),
    ]
    for load in loads:
        load.start()
    pl.semaphore_wait(barrier, 5)

    def y_copy(k):
        return pltpu.make_async_remote_copy(
            src_ref=coef_hbm.at[:, k], dst_ref=from_y.at[:, k], send_sem=ysend.at[k], recv_sem=yrecv.at[k],
            device_id=(grp, dev_y), device_id_type=MESH,
        )

    def z_copy(k):
        return pltpu.make_async_remote_copy(
            src_ref=to_z.at[k], dst_ref=from_z.at[k], send_sem=zsend.at[k], recv_sem=zrecv.at[k],
            device_id=(grp, dev_z), device_id_type=MESH,
        )

    def g_copy(k, which):
        return pltpu.make_async_remote_copy(
            src_ref=packed.at[k], dst_ref=gathered.at[which, k], send_sem=gsend.at[which, k],
            recv_sem=grecv.at[which, k], device_id=(peers[which], dev), device_id_type=MESH,
        )

    for k in range(rhs):
        y_copy(k).start()

    shape = (8, LANES)
    lane = lax.broadcasted_iota(jnp.int32, shape, 1)
    row = lax.broadcasted_iota(jnp.int32, shape, 0)
    quarter = LANES // 4
    u2 = lane // quarter
    place = lane % quarter
    space_root = jnp.zeros(shape, jnp.int32)
    wave_root = jnp.zeros(shape, jnp.int32)
    for r in range(quarter):
        space_root = jnp.where(place == r, space_ref[height * quarter + r], space_root)
        wave_root = jnp.where(place == r, wave_ref[height * quarter + r], wave_root)
    coarse_space = LEVELS // 2 - 1
    coarse_wave = LEVELS // 2 - 2
    places = [u0, grp % 4, u2]
    z_col = jnp.full(shape, float(NODES[0]), jnp.float32)
    for i in range(1, 8):
        z_col = jnp.where(row == i, jnp.float32(NODES[i]), z_col)

    def space_box(section, first):
        one = lax.shift_right_logical(space_root, jnp.int32(coarse_space))
        two = lax.bitwise_and(space_root, jnp.int32(2**coarse_space - 1))
        for position in range(section):
            digit = first if position == 0 else places[position]
            one = 2 * one + digit % 2
            two = 2 * two + digit // 2
        side = 0.5 ** (coarse_space + section)
        return one.astype(jnp.float32) * side, two.astype(jnp.float32) * side, side

    def wave_box(section, first):
        one = lax.shift_right_logical(wave_root, jnp.int32(coarse_wave))
        two = lax.bitwise_and(wave_root, jnp.int32(2**coarse_wave - 1))
        for position in range(2, section - 1, -1):
            digit = first if position == 0 else places[position]
            one = 2 * one + digit % 2
            two = 2 * two + digit // 2
        side = float(2**LEVELS) / float(2 ** (coarse_wave + 3 - section))
        start = -0.5 * float(2**LEVELS)
        return start + one.astype(jnp.float32) * side, start + two.astype(jnp.float32) * side, side

    def center(box):
        return box[0] + 0.5 * box[2], box[1] + 0.5 * box[2]

    def axis_points(box, i1):
        return box[0] + box[2] * float(NODES[i1]), box[1] + box[2] * z_col

    targets = [u0, flip(u0, 2)]
    children = [u0, flip(u0, 1)]
    for ti in range(2):
        a1, a2 = center(space_box(1, targets[ti]))
        sq1, sq2 = speeds(a1, a2)
        for ci in range(2):
            box = wave_box(0, children[ci])
            for i1 in range(8):
                k1, k2 = axis_points(box, i1)
                cosine, sine = cos_sin(turns_of(a1, a2, sq1, sq2, k1, k2))
                rot_c[ti, ci, pl.ds(8 * i1, 8), :] = cosine
                rot_s[ti, ci, pl.ds(8 * i1, 8), :] = sine
        if ti == 0:
            box = wave_box(1, u0)
            for i1 in range(8):
                k1, k2 = axis_points(box, i1)
                pre_turn[pl.ds(8 * i1, 8), :] = frac(turns_of(a1, a2, sq1, sq2, k1, k2))
    space_1 = space_box(1, u0)
    wave_1 = wave_box(1, u0)
    b1, b2 = center(wave_1)
    space_3 = space_box(3, u0)
    d1, d2 = center(wave_box(3, u0))
    for i1 in range(8):
        x1, x2 = axis_points(space_1, i1)
        sq1, sq2 = speeds(x1, x2)
        x_rows[0, i1] = x1
        x_rows[1, i1] = sq1
        x_rows[2, i1] = sq2
        x_rows[3, i1] = frac(turns_of(x1, x2, sq1, sq2, b1, b2))
        k2 = wave_1[1] + wave_1[2] * float(NODES[i1])
        k1 = wave_1[0] + wave_1[2] * float(NODES[i1])
        x2k2[i1] = x2 * k2
        k_rows[0, i1] = k1
        k_rows[1, i1] = k2 * k2
        x1, x2 = axis_points(space_3, i1)
        sq1, sq2 = speeds(x1, x2)
        cosine, sine = cos_sin(turns_of(x1, x2, sq1, sq2, d1, d2))
        fin_c[pl.ds(8 * i1, 8), :] = cosine
        fin_s[pl.ds(8 * i1, 8), :] = sine

    def kernel_rows(tb):
        x1 = x_rows[0, tb]
        sq1 = x_rows[1, tb]
        sq2 = x_rows[2, tb]
        turn = x_rows[3, tb]
        second = [sq2 * k_rows[1, s2] for s2 in range(8)]
        for s1 in range(8):
            k1 = k_rows[0, s1]
            first = sq1 * (k1 * k1)
            line = x1 * k1
            for s2 in range(8):
                s = 8 * s1 + s2
                angle = (line + x2k2[s2]) + root_of(first + second[s2])
                extra = jnp.broadcast_to(pre_turn[pl.ds(s, 1), :], shape) - turn
                cosine, sine = cos_sin(frac(angle) + extra, 1.0 / 64.0)
                ker_c[tb, s] = cosine
                ker_s[tb, s] = sine

    def stage_b(k):
        copy = y_copy(k)
        copy.wait_recv()
        for ci in range(2):
            held = own if ci == 0 else from_y
            real, imag = held[0, k], held[1, k]
            for ti in range(2):
                cosine, sine = rot_c[ti, ci], rot_s[ti, ci]
                for a, value in enumerate([real * cosine + imag * sine, imag * cosine - real * sine]):
                    high, low = split(value)
                    columns = pl.ds((2 * ti + a) * LANES, LANES)
                    rhs_pre[pl.ds(64 * ci, 64), columns] = high
                    rhs_pre[pl.ds(128 + 64 * ci, 64), columns] = low
        for ti in (1, 0):
            product = jnp.dot(
                pre_tab[...], rhs_pre[:, 2 * ti * LANES : (2 * ti + 2) * LANES],
                preferred_element_type=jnp.float32,
            )
            total = product[:64] + product[64:]
            place_of = to_z if ti == 1 else part
            place_of[k, 0] = total[:, :LANES]
            place_of[k, 1] = total[:, LANES:]
            if ti == 1:
                z_copy(k).start()

    group_16 = lax.broadcasted_iota(jnp.int32, (16, LANES), 1) // quarter

    def stage_c(k):
        z_copy(k).wait_recv()
        spread[...] = part[k] + from_z[k]

        def body(outer, sums):
            sums = list(sums)
            for inner in range(8):
                s = 8 * outer + inner
                real = jnp.broadcast_to(spread[0, pl.ds(s, 1), :], shape)
                imag = jnp.broadcast_to(spread[1, pl.ds(s, 1), :], shape)
                for tb in range(8):
                    cosine, sine = ker_c[tb, s], ker_s[tb, s]
                    sums[2 * tb] += cosine * real - sine * imag
                    sums[2 * tb + 1] += sine * real + cosine * imag
            return tuple(sums)

        sums = lax.fori_loop(0, 8, body, tuple(jnp.zeros(shape, jnp.float32) for _ in range(16)))
        for a in range(2):
            sets = [jnp.concatenate([sums[4 * g + a], sums[4 * g + 2 + a]], axis=0) for g in range(4)]
            total = None
            for d in range(4):
                chosen = sets[(3 - d) % 4]
                for g in range(3):
                    chosen = jnp.where(group_16 == g, sets[(g - d) % 4], chosen)
                if d:
                    chosen = pltpu.roll(chosen, LANES - quarter * d, 1)
                total = chosen if total is None else total + chosen
            packed[k, a] = total
        for which in range(3):
            g_copy(k, which).start()

    def stage_e(k):
        for which in range(3):
            g_copy(k, which).wait_recv()
        for a in range(2):
            total = (packed[k, a] + gathered[0, k, a]) + (gathered[1, k, a] + gathered[2, k, a])
            high = total.astype(jnp.bfloat16).astype(jnp.float32)
            for level, value in enumerate([high, total - high]):
                rolled = [value] + [pltpu.roll(value, quarter * d, 1) for d in range(1, 4)]
                for j in range(4):
                    for g in range(4):
                        rows = pl.ds(256 * level + 64 * j + 16 * g, 16)
                        rhs_last[rows, pl.ds(a * LANES, LANES)] = jnp.where(
                            group_16 == j, rolled[(j - g) % 4], 0.0
                        ).astype(jnp.bfloat16)
        product = jnp.dot(last_tab[...], rhs_last[...], preferred_element_type=jnp.float32)
        total = product[:64] + product[64:]
        real, imag = total[:, :LANES], total[:, LANES:]
        cosine, sine = fin_c[...], fin_s[...]
        out_ref[0, k] = real * cosine - imag * sine
        out_ref[1, k] = real * sine + imag * cosine

    for load in loads:
        load.wait()

    per_step = 8 // K_STEPS

    def step(i, carry):
        @pl.when(i < K_STEPS)
        def _():
            def rows(j, inner):
                kernel_rows(i * per_step + j)
                return inner

            lax.fori_loop(0, per_step, rows, 0)

        @pl.when(i < rhs)
        def _():
            stage_b(i)

        @pl.when(jnp.logical_and(i >= LAG_C, i < LAG_C + rhs))
        def _():
            stage_c(i - LAG_C)

        @pl.when(i >= LAG_E)
        def _():
            stage_e(i - LAG_E)

        return carry

    lax.fori_loop(0, rhs + LAG_E, step, 0)
    for k in range(rhs):
        y_copy(k).wait_send()
        z_copy(k).wait_send()
        for which in range(3):
            g_copy(k, which).wait_send()


def per_device(coefficients, spatial_root, frequency_root):
    _, rhs, rank, pairs = coefficients.shape
    block = (2, rhs, rank, pairs)
    f32 = jnp.float32
    hbm = pl.BlockSpec(memory_space=pl.ANY)
    smem = pl.BlockSpec(memory_space=pltpu.SMEM)
    vmem = pl.BlockSpec(memory_space=pltpu.VMEM)
    tile = (8, LANES)
    table = (rank, LANES)
    dma = pltpu.SemaphoreType.DMA
    return pl.pallas_call(
        kernel,
        name="butterfly",
        out_shape=jax.ShapeDtypeStruct(block, f32),
        in_specs=[smem, smem, hbm, hbm, hbm],
        out_specs=vmem,
        scratch_shapes=[
            pltpu.VMEM(block, f32),
            pltpu.VMEM(block, f32),
            pltpu.VMEM((rhs, 2) + table, f32),
            pltpu.VMEM((rhs, 2) + table, f32),
            pltpu.VMEM((rhs, 2) + table, f32),
            pltpu.VMEM((rhs, 2, 16, LANES), f32),
            pltpu.VMEM((3, rhs, 2, 16, LANES), f32),
            pltpu.VMEM(PRE_TABLE.shape[1:], jnp.bfloat16),
            pltpu.VMEM(LAST_TABLE.shape[1:], jnp.bfloat16),
            pltpu.VMEM((2, 2) + table, f32),
            pltpu.VMEM((2, 2) + table, f32),
            pltpu.VMEM((8, rank) + tile, f32),
            pltpu.VMEM((8, rank) + tile, f32),
            pltpu.VMEM(table, f32),
            pltpu.VMEM(table, f32),
            pltpu.VMEM(table, f32),
            pltpu.VMEM((2,) + table, f32),
            pltpu.VMEM((4, 8) + tile, f32),
            pltpu.VMEM((8,) + tile, f32),
            pltpu.VMEM((2, 8) + tile, f32),
            pltpu.VMEM((256, 4 * LANES), jnp.bfloat16),
            pltpu.VMEM((512, 2 * LANES), jnp.bfloat16),
            dma((3,)),
            dma((rhs,)),
            dma((rhs,)),
            dma((rhs,)),
            dma((rhs,)),
            dma((3, rhs)),
            dma((3, rhs)),
        ],
        compiler_params=pltpu.CompilerParams(
            collective_id=0, has_side_effects=True, vmem_limit_bytes=32 * 2**20
        ),
    )(spatial_root, frequency_root, coefficients, jnp.asarray(PRE_TABLE), jnp.asarray(LAST_TABLE))


def solution(mesh):
    return jax.shard_map(
        per_device,
        mesh=mesh,
        in_specs=(P(None, None, None, ("grp", "dev")), P(), P()),
        out_specs=P(None, None, None, ("grp", "dev")),
        check_vma=False,
    )
```

time: 218 us -> 32.8 us (0.15)
  matrix products: 121 us -> 0 us
  waiting for transfers between devices: 64 us -> 0 us
  Pallas kernels: 0 us -> 27.4 us
  between operations: 14 us -> 0.01 us
  other arithmetic: 10 us -> 0 us
  starting transfers between devices: 4.86 us -> 0 us
    dot_general x7 -> x0, matrix products: 121 us -> none  [the longest x1 29 us: switch_step(): jnp.einsum('tsm,ksm->ktm', cosine, values[1], precision=HIGHEST)]
    psum x1 -> x0, waiting for transfers between devices: 36.7 us -> none  [per_device(): lax.psum(terms, 'grp')]
    pallas_call x0 -> x1, Pallas kernels: none -> 27.4 us  [per_device(): pl.pallas_call(kernel, name='butterfly', out_shape=jax.ShapeDtypeStruct(b...]
    ppermute x2 -> x0, waiting for transfers between devices: 27.3 us -> none  [partner_2(): return lax.ppermute(block, axis, route)]
    unnamed x3 -> x11, local copies, waits for them, and re-layouts: 0.01 us -> 5.14 us
    ppermute x2 -> x0, starting transfers between devices: 4.86 us -> none  [partner_2(): return lax.ppermute(block, axis, route)]
    cos x4 -> x0, other arithmetic: 2.32 us -> none  [rotate(): cosine = jnp.cos(turn_angle)]
  transfers between devices with their start and end apart: 3 -> 0, of which waited for: 3 -> 0; matrix products, arithmetic and copies ran while one was open for 4% -> 0% of each run, Pallas kernels for 0% -> 0%
where the time goes in v1:
time: 32.8 us; the launch traced here: 32.6 us
  Pallas kernels  27.4 us (84%)
  local copies, waits for them, and re-layouts  5.14 us (16%)
    pallas_call x1, Pallas kernels, per_device(): pl.pallas_call(kernel, name='butterfly', out_shape=jax.ShapeDtypeStruct(b...  27.4 us
    unnamed x11, local copies, waits for them, and re-layouts  5.14 us

profile of v1, /device:TPU:0, one launch (start us, length us, event | category | flops | bytes accessed | tf_op | source)
XLA Modules:
  0.0 32.6 jit_solution(396718268324787957)
XLA Ops:
  0.0 0.0 copy-start
  0.0 1.0 %copy-done = f32[2,8,64,128]{3,2,1,0:T(8,128)S(1)} copy-done((f32[2,8,64,128]{3,2,1,0:T(8,128)S(1)}, f32[2,8,64,128]{3,2,1,0:T(8,128)}, u32[]{:S(2)}) %copy-start) | copy-done | bytes 524312
  1.0 0.0 copy-start.1
  1.0 1.0 %copy-done.1 = bf16[4,128,512]{2,1,0:T(8,128)(2,1)S(1)} copy-done((bf16[4,128,512]{2,1,0:T(8,128)(2,1)S(1)}, bf16[4,128,512]{2,1,0:T(8,128)(2,1)}, u32[]{:S(2)}) %copy-start.1) | copy-done | bytes 524312
  2.1 0.0 copy-start.2
  2.1 0.9 %copy-done.2 = bf16[4,128,256]{2,1,0:T(8,128)(2,1)S(1)} copy-done((bf16[4,128,256]{2,1,0:T(8,128)(2,1)S(1)}, bf16[4,128,256]{2,1,0:T(8,128)(2,1)}, u32[]{:S(2)}) %copy-start.2) | copy-done | bytes 262168
  3.0 0.0 copy-start.3
  3.0 0.7 %copy-done.3 = s32[64]{0:T(128)S(1)} copy-done((s32[64]{0:T(128)S(1)}, s32[64]{0:T(128)}, u32[]{:S(2)}) %copy-start.3) | copy-done | bytes 280
  3.7 0.0 copy-start.4
  3.7 0.7 %copy-done.4 = s32[64]{0:T(128)S(1)} copy-done((s32[64]{0:T(128)S(1)}, s32[64]{0:T(128)}, u32[]{:S(2)}) %copy-start.4) | copy-done | bytes 280
  4.3 27.4 %butterfly.1 = f32[2,8,64,128]{3,2,1,0:T(8,128)S(1)} custom-call(s32[64]{0:T(128)S(1)} %copy-done.3, s32[64]{0:T(128)S(1)} %copy-done.4, f32[2,8,64,128]{3,2,1,0:T(8,128)S(1)} %copy-done, bf16[4,128,256]{2,1,0:T(8,128)(2,1)S(1)} %copy-done.2, bf16[4,128,512]{2,1,0:T(8,128)(2,1)S(1)} %copy-done.1), custom_call_target="tpu_custom_call" | custom-call | tf_op jit(solution)/shard_map/butterfly/pallas_call | solution.py:388
  31.8 0.8 %copy.7 = f32[2,8,64,128]{3,2,1,0:T(8,128)} copy(f32[2,8,64,128]{3,2,1,0:T(8,128)S(1)} %butterfly.1) | data formatting | bytes 1048576
Async XLA Ops:
  0.0 1.0 %copy-start = (f32[2,8,64,128]{3,2,1,0:T(8,128)S(1)}, f32[2,8,64,128]{3,2,1,0:T(8,128)}, u32[]{:S(2)}) copy-start(f32[2,8,64,128]{3,2,1,0:T(8,128)} %coef_hbm.1) | copy-start | bytes 1572868
  1.0 1.0 %copy-start.1 = (bf16[4,128,512]{2,1,0:T(8,128)(2,1)S(1)}, bf16[4,128,512]{2,1,0:T(8,128)(2,1)}, u32[]{:S(2)}) copy-start(bf16[4,128,512]{2,1,0:T(8,128)(2,1)} %constant.5.clone.last_hbm) | copy-start | bytes 1572868
  2.1 0.9 %copy-start.2 = (bf16[4,128,256]{2,1,0:T(8,128)(2,1)S(1)}, bf16[4,128,256]{2,1,0:T(8,128)(2,1)}, u32[]{:S(2)}) copy-start(bf16[4,128,256]{2,1,0:T(8,128)(2,1)} %constant.4.clone.pre_hbm) | copy-start | bytes 786436
  3.0 0.7 %copy-start.3 = (s32[64]{0:T(128)S(1)}, s32[64]{0:T(128)}, u32[]{:S(2)}) copy-start(s32[64]{0:T(128)} %space_ref.1) | copy-start | bytes 772
  3.7 0.7 %copy-start.4 = (s32[64]{0:T(128)S(1)}, s32[64]{0:T(128)}, u32[]{:S(2)}) copy-start(s32[64]{0:T(128)} %wave_ref.1) | copy-start | bytes 772

commit v2 on v1

--- a/solution.py
+++ b/solution.py
@@ -13,9 +13,11 @@
 LEVELS = 12
 MESH = pl.DeviceIdType.MESH
 LANES = 128
-K_STEPS = 4
-LAG_C = 3
-LAG_E = 5
+K_PLAN = (2, 3, 3)
+AHEAD = 3
+LAG_C = 2
+LAG_E = 4
+UNROLL = 8
 
 NODES = 0.5 - 0.5 * np.cos(np.pi * (2.0 * np.arange(8) + 1.0) / 16.0)
 
@@ -42,7 +44,10 @@
 
 
 PRE_TABLE = np.stack(
-    [split_table(np.concatenate([INTERP[u].T, INTERP[u ^ 1].T], axis=1)) for u in range(4)]
+    [
+        np.stack([split_table(np.concatenate([INTERP[u].T, INTERP[u ^ bit].T], axis=1)) for bit in (1, 2)])
+        for u in range(4)
+    ]
 )
 LAST_TABLE = np.stack(
     [split_table(np.concatenate([INTERP[j] @ INTERP[u] for j in range(4)], axis=1)) for u in range(4)]
@@ -109,11 +114,11 @@
 
 
 def kernel(
-    space_ref, wave_ref, coef_hbm, pre_hbm, last_hbm, out_ref,
-    own, from_y, to_z, from_z, part, packed, gathered,
-    pre_tab, last_tab, rot_c, rot_s, ker_c, ker_s, pre_turn, fin_c, fin_s, spread,
+    space_hbm, wave_hbm, coef_hbm, pre_hbm, last_hbm, out_ref,
+    own, from_first, to_second, from_second, part, packed, gathered,
+    pre_tab, last_tab, rot_c, rot_s, ker, pre_turn, fin_c, fin_s, spread,
     x_rows, x2k2, k_rows, rhs_pre, rhs_last,
-    load_sem, ysend, yrecv, zsend, zrecv, gsend, grecv,
+    space_ref, wave_ref, load_sem, fsend, frecv, ssend, srecv, gsend, grecv,
 ):
     rhs = coef_hbm.shape[1]
     grp = lax.axis_index("grp")
@@ -127,35 +132,44 @@
     barrier = pltpu.get_barrier_semaphore()
     for target in [(grp, dev_y), (grp, dev_z)] + [(peer, dev) for peer in peers]:
         pl.semaphore_signal(barrier, inc=1, device_id=target, device_id_type=MESH)
+    roots = [
+        pltpu.make_async_copy(space_hbm, space_ref, load_sem.at[3]),
+        pltpu.make_async_copy(wave_hbm, wave_ref, load_sem.at[4]),
+    ]
     loads = [
         pltpu.make_async_copy(coef_hbm, own, load_sem.at[0]),
         pltpu.make_async_copy(pre_hbm.at[u0], pre_tab, load_sem.at[1]),
         pltpu.make_async_copy(last_hbm.at[grp], last_tab, load_sem.at[2]),
     ]
-    for load in loads:
+    for load in roots + loads:
         load.start()
     pl.semaphore_wait(barrier, 5)
 
-    def y_copy(k):
+    across = [dev_y, dev_z]
+
+    def first_copy(k):
         return pltpu.make_async_remote_copy(
-            src_ref=coef_hbm.at[:, k], dst_ref=from_y.at[:, k], send_sem=ysend.at[k], recv_sem=yrecv.at[k],
-            device_id=(grp, dev_y), device_id_type=MESH,
+            src_ref=coef_hbm.at[:, k], dst_ref=from_first.at[:, k], send_sem=fsend.at[k], recv_sem=frecv.at[k],
+            device_id=(grp, across[k % 2]), device_id_type=MESH,
         )
 
-    def z_copy(k):
+    def second_copy(k):
         return pltpu.make_async_remote_copy(
-            src_ref=to_z.at[k], dst_ref=from_z.at[k], send_sem=zsend.at[k], recv_sem=zrecv.at[k],
-            device_id=(grp, dev_z), device_id_type=MESH,
+            src_ref=to_second.at[k], dst_ref=from_second.at[k], send_sem=ssend.at[k], recv_sem=srecv.at[k],
+            device_id=(grp, across[1 - k % 2]), device_id_type=MESH,
         )
 
-    def g_copy(k, which):
+    def g_copy(j, which):
         return pltpu.make_async_remote_copy(
-            src_ref=packed.at[k], dst_ref=gathered.at[which, k], send_sem=gsend.at[which, k],
-            recv_sem=grecv.at[which, k], device_id=(peers[which], dev), device_id_type=MESH,
+            src_ref=packed.at[j], dst_ref=gathered.at[which, j], send_sem=gsend.at[which, j],
+            recv_sem=grecv.at[which, j], device_id=(peers[which], dev), device_id_type=MESH,
         )
 
-    for k in range(rhs):
-        y_copy(k).start()
+    for k in range(2 * AHEAD):
+        first_copy(k).start()
+
+    for root in roots:
+        root.wait()
 
     shape = (8, LANES)
     lane = lax.broadcasted_iota(jnp.int32, shape, 1)
@@ -202,18 +216,19 @@
     def axis_points(box, i1):
         return box[0] + box[2] * float(NODES[i1]), box[1] + box[2] * z_col
 
-    targets = [u0, flip(u0, 2)]
-    children = [u0, flip(u0, 1)]
-    for ti in range(2):
-        a1, a2 = center(space_box(1, targets[ti]))
+    near, far = flip(u0, 1), flip(u0, 2)
+    plan = [(u0, [(0, u0), (1, near), (4, far)]), (far, [(2, u0), (3, near)]), (near, [(5, u0), (6, far)])]
+    rotation = [[[0, 1], [2, 3]], [[0, 4], [5, 6]]]
+    for ti, (target, children) in enumerate(plan):
+        a1, a2 = center(space_box(1, target))
         sq1, sq2 = speeds(a1, a2)
-        for ci in range(2):
-            box = wave_box(0, children[ci])
+        for ri, child in children:
+            box = wave_box(0, child)
             for i1 in range(8):
                 k1, k2 = axis_points(box, i1)
                 cosine, sine = cos_sin(turns_of(a1, a2, sq1, sq2, k1, k2))
-                rot_c[ti, ci, pl.ds(8 * i1, 8), :] = cosine
-                rot_s[ti, ci, pl.ds(8 * i1, 8), :] = sine
+                rot_c[ri, pl.ds(8 * i1, 8), :] = cosine
+                rot_s[ri, pl.ds(8 * i1, 8), :] = sine
         if ti == 0:
             box = wave_box(1, u0)
             for i1 in range(8):
@@ -257,130 +272,140 @@
                 angle = (line + x2k2[s2]) + root_of(first + second[s2])
                 extra = jnp.broadcast_to(pre_turn[pl.ds(s, 1), :], shape) - turn
                 cosine, sine = cos_sin(frac(angle) + extra, 1.0 / 64.0)
-                ker_c[tb, s] = cosine
-                ker_s[tb, s] = sine
+                ker[0, tb, s] = cosine
+                ker[1, tb, s] = sine - cosine
+                ker[2, tb, s] = sine + cosine
 
     def stage_b(k):
-        copy = y_copy(k)
-        copy.wait_recv()
+        kind = k % 2
+        first_copy(k).wait_recv()
         for ci in range(2):
-            held = own if ci == 0 else from_y
+            held = own if ci == 0 else from_first
             real, imag = held[0, k], held[1, k]
             for ti in range(2):
-                cosine, sine = rot_c[ti, ci], rot_s[ti, ci]
+                ri = rotation[kind][ti][ci]
+                cosine, sine = rot_c[ri], rot_s[ri]
                 for a, value in enumerate([real * cosine + imag * sine, imag * cosine - real * sine]):
                     high, low = split(value)
                     columns = pl.ds((2 * ti + a) * LANES, LANES)
-                    rhs_pre[pl.ds(64 * ci, 64), columns] = high
-                    rhs_pre[pl.ds(128 + 64 * ci, 64), columns] = low
+                    rhs_pre[kind, pl.ds(64 * ci, 64), columns] = high
+                    rhs_pre[kind, pl.ds(128 + 64 * ci, 64), columns] = low
         for ti in (1, 0):
             product = jnp.dot(
-                pre_tab[...], rhs_pre[:, 2 * ti * LANES : (2 * ti + 2) * LANES],
+                pre_tab[kind], rhs_pre[kind, :, 2 * ti * LANES : (2 * ti + 2) * LANES],
                 preferred_element_type=jnp.float32,
             )
             total = product[:64] + product[64:]
-            place_of = to_z if ti == 1 else part
+            place_of = to_second if ti == 1 else part
             place_of[k, 0] = total[:, :LANES]
             place_of[k, 1] = total[:, LANES:]
             if ti == 1:
-                z_copy(k).start()
+                second_copy(k).start()
 
     group_16 = lax.broadcasted_iota(jnp.int32, (16, LANES), 1) // quarter
 
-    def stage_c(k):
-        z_copy(k).wait_recv()
-        spread[...] = part[k] + from_z[k]
+    def stage_c(j):
+        for e in range(2):
+            k = 2 * j + e
+            second_copy(k).wait_recv()
+            real = part[k, 0] + from_second[k, 0]
+            imag = part[k, 1] + from_second[k, 1]
+            spread[e, 0] = real + imag
+            spread[e, 1] = real
+            spread[e, 2] = imag
 
         def body(outer, sums):
             sums = list(sums)
-            for inner in range(8):
-                s = 8 * outer + inner
-                real = jnp.broadcast_to(spread[0, pl.ds(s, 1), :], shape)
-                imag = jnp.broadcast_to(spread[1, pl.ds(s, 1), :], shape)
+            for inner in range(UNROLL):
+                s = UNROLL * outer + inner
+                rows = [[jnp.broadcast_to(spread[e, q, pl.ds(s, 1), :], shape) for q in range(3)] for e in range(2)]
                 for tb in range(8):
-                    cosine, sine = ker_c[tb, s], ker_s[tb, s]
-                    sums[2 * tb] += cosine * real - sine * imag
-                    sums[2 * tb + 1] += sine * real + cosine * imag
+                    for q in range(3):
+                        entry = ker[q, tb, s]
+                        for e in range(2):
+                            sums[24 * e + 3 * tb + q] += entry * rows[e][q]
             return tuple(sums)
 
-        sums = lax.fori_loop(0, 8, body, tuple(jnp.zeros(shape, jnp.float32) for _ in range(16)))
-        for a in range(2):
-            sets = [jnp.concatenate([sums[4 * g + a], sums[4 * g + 2 + a]], axis=0) for g in range(4)]
-            total = None
-            for d in range(4):
-                chosen = sets[(3 - d) % 4]
-                for g in range(3):
-                    chosen = jnp.where(group_16 == g, sets[(g - d) % 4], chosen)
-                if d:
-                    chosen = pltpu.roll(chosen, LANES - quarter * d, 1)
-                total = chosen if total is None else total + chosen
-            packed[k, a] = total
+        sums = lax.fori_loop(0, 64 // UNROLL, body, tuple(jnp.zeros(shape, jnp.float32) for _ in range(48)))
+        for e in range(2):
+            three = [sums[24 * e + 3 * tb : 24 * e + 3 * tb + 3] for tb in range(8)]
+            for a, parts in enumerate([[p[0] - p[2] for p in three], [p[0] + p[1] for p in three]]):
+                sets = [jnp.concatenate([parts[2 * g], parts[2 * g + 1]], axis=0) for g in range(4)]
+                total = None
+                for d in range(4):
+                    chosen = sets[(3 - d) % 4]
+                    for g in range(3):
+                        chosen = jnp.where(group_16 == g, sets[(g - d) % 4], chosen)
+                    if d:
+                        chosen = pltpu.roll(chosen, LANES - quarter * d, 1)
+                    total = chosen if total is None else total + chosen
+                packed[j, e, a] = total
+        for which in (2, 1, 0):
+            g_copy(j, which).start()
+
+    def stage_e(j):
         for which in range(3):
-            g_copy(k, which).start()
-
-    def stage_e(k):
-        for which in range(3):
-            g_copy(k, which).wait_recv()
-        for a in range(2):
-            total = (packed[k, a] + gathered[0, k, a]) + (gathered[1, k, a] + gathered[2, k, a])
-            high = total.astype(jnp.bfloat16).astype(jnp.float32)
-            for level, value in enumerate([high, total - high]):
-                rolled = [value] + [pltpu.roll(value, quarter * d, 1) for d in range(1, 4)]
-                for j in range(4):
-                    for g in range(4):
-                        rows = pl.ds(256 * level + 64 * j + 16 * g, 16)
-                        rhs_last[rows, pl.ds(a * LANES, LANES)] = jnp.where(
-                            group_16 == j, rolled[(j - g) % 4], 0.0
-                        ).astype(jnp.bfloat16)
+            g_copy(j, which).wait_recv()
+        for e in range(2):
+            for a in range(2):
+                total = (packed[j, e, a] + gathered[0, j, e, a]) + (gathered[1, j, e, a] + gathered[2, j, e, a])
+                high = total.astype(jnp.bfloat16).astype(jnp.float32)
+                for level, value in enumerate([high, total - high]):
+                    rolled = [value] + [pltpu.roll(value, quarter * d, 1) for d in range(1, 4)]
+                    for jj in range(4):
+                        for g in range(4):
+                            rows = pl.ds(256 * level + 64 * jj + 16 * g, 16)
+                            rhs_last[rows, pl.ds((2 * e + a) * LANES, LANES)] = jnp.where(
+                                group_16 == jj, rolled[(jj - g) % 4], 0.0
+                            ).astype(jnp.bfloat16)
         product = jnp.dot(last_tab[...], rhs_last[...], preferred_element_type=jnp.float32)
         total = product[:64] + product[64:]
-        real, imag = total[:, :LANES], total[:, LANES:]
         cosine, sine = fin_c[...], fin_s[...]
-        out_ref[0, k] = real * cosine - imag * sine
-        out_ref[1, k] = real * sine + imag * cosine
-
+        for e in range(2):
+            real = total[:, 2 * e * LANES : (2 * e + 1) * LANES]
+            imag = total[:, (2 * e + 1) * LANES : (2 * e + 2) * LANES]
+            out_ref[0, 2 * j + e] = real * cosine - imag * sine
+            out_ref[1, 2 * j + e] = real * sine + imag * cosine
+
+    k_ends = np.cumsum((0,) + K_PLAN)
+
+    def kernel_part(part_id):
+        def rows(tb, inner):
+            kernel_rows(tb)
+            return inner
+
+        if part_id < len(K_PLAN):
+            lax.fori_loop(int(k_ends[part_id]), int(k_ends[part_id + 1]), rows, 0)
+
+    kernel_part(0)
+    pairs = rhs // 2
     for load in loads:
         load.wait()
-
-    per_step = 8 // K_STEPS
-
-    def step(i, carry):
-        @pl.when(i < K_STEPS)
-        def _():
-            def rows(j, inner):
-                kernel_rows(i * per_step + j)
-                return inner
-
-            lax.fori_loop(0, per_step, rows, 0)
-
-        @pl.when(i < rhs)
-        def _():
-            stage_b(i)
-
-        @pl.when(jnp.logical_and(i >= LAG_C, i < LAG_C + rhs))
-        def _():
+    for i in range(pairs + LAG_E):
+        if i < pairs:
+            for e in range(2):
+                stage_b(2 * i + e)
+            if i + AHEAD < pairs:
+                for e in range(2):
+                    first_copy(2 * (i + AHEAD) + e).start()
+        kernel_part(i + 1)
+        if 0 <= i - LAG_C < pairs:
             stage_c(i - LAG_C)
-
-        @pl.when(i >= LAG_E)
-        def _():
+        if i >= LAG_E:
             stage_e(i - LAG_E)
-
-        return carry
-
-    lax.fori_loop(0, rhs + LAG_E, step, 0)
     for k in range(rhs):
-        y_copy(k).wait_send()
-        z_copy(k).wait_send()
+        first_copy(k).wait_send()
+        second_copy(k).wait_send()
+    for j in range(pairs):
         for which in range(3):
-            g_copy(k, which).wait_send()
+            g_copy(j, which).wait_send()
 
 
 def per_device(coefficients, spatial_root, frequency_root):
     _, rhs, rank, pairs = coefficients.shape
     block = (2, rhs, rank, pairs)
     f32 = jnp.float32
-    hbm = pl.BlockSpec(memory_space=pl.ANY)
-    smem = pl.BlockSpec(memory_space=pltpu.SMEM)
+    hbm = pl.BlockSpec(memory_space=pltpu.HBM)
     vmem = pl.BlockSpec(memory_space=pltpu.VMEM)
     tile = (8, LANES)
     table = (rank, LANES)
@@ -389,7 +414,7 @@
         kernel,
         name="butterfly",
         out_shape=jax.ShapeDtypeStruct(block, f32),
-        in_specs=[smem, smem, hbm, hbm, hbm],
+        in_specs=[hbm] * 5,
         out_specs=vmem,
         scratch_shapes=[
             pltpu.VMEM(block, f32),
@@ -397,33 +422,34 @@
             pltpu.VMEM((rhs, 2) + table, f32),
             pltpu.VMEM((rhs, 2) + table, f32),
             pltpu.VMEM((rhs, 2) + table, f32),
-            pltpu.VMEM((rhs, 2, 16, LANES), f32),
-            pltpu.VMEM((3, rhs, 2, 16, LANES), f32),
+            pltpu.VMEM((rhs // 2, 2, 2, 16, LANES), f32),
+            pltpu.VMEM((3, rhs // 2, 2, 2, 16, LANES), f32),
             pltpu.VMEM(PRE_TABLE.shape[1:], jnp.bfloat16),
             pltpu.VMEM(LAST_TABLE.shape[1:], jnp.bfloat16),
-            pltpu.VMEM((2, 2) + table, f32),
-            pltpu.VMEM((2, 2) + table, f32),
-            pltpu.VMEM((8, rank) + tile, f32),
-            pltpu.VMEM((8, rank) + tile, f32),
+            pltpu.VMEM((7,) + table, f32),
+            pltpu.VMEM((7,) + table, f32),
+            pltpu.VMEM((3, 8, rank) + tile, f32),
             pltpu.VMEM(table, f32),
             pltpu.VMEM(table, f32),
             pltpu.VMEM(table, f32),
-            pltpu.VMEM((2,) + table, f32),
+            pltpu.VMEM((2, 3) + table, f32),
             pltpu.VMEM((4, 8) + tile, f32),
             pltpu.VMEM((8,) + tile, f32),
             pltpu.VMEM((2, 8) + tile, f32),
-            pltpu.VMEM((256, 4 * LANES), jnp.bfloat16),
-            pltpu.VMEM((512, 2 * LANES), jnp.bfloat16),
-            dma((3,)),
+            pltpu.VMEM((2, 256, 4 * LANES), jnp.bfloat16),
+            pltpu.VMEM((512, 4 * LANES), jnp.bfloat16),
+            pltpu.SMEM(spatial_root.shape, jnp.int32),
+            pltpu.SMEM(frequency_root.shape, jnp.int32),
+            dma((5,)),
             dma((rhs,)),
             dma((rhs,)),
             dma((rhs,)),
             dma((rhs,)),
-            dma((3, rhs)),
-            dma((3, rhs)),
+            dma((3, rhs // 2)),
+            dma((3, rhs // 2)),
         ],
         compiler_params=pltpu.CompilerParams(
-            collective_id=0, has_side_effects=True, vmem_limit_bytes=32 * 2**20
+            collective_id=0, has_side_effects=True, vmem_limit_bytes=60 * 2**20
         ),
     )(spatial_root, frequency_root, coefficients, jnp.asarray(PRE_TABLE), jnp.asarray(LAST_TABLE))
 

time: 32.8 us -> 26.3 us (0.80)
  local copies, waits for them, and re-layouts: 5.14 us -> 1.89 us
  Pallas kernels: 27.4 us -> 24.3 us
    unnamed x11 -> x1, local copies, waits for them, and re-layouts: 5.14 us -> 1.89 us
    pallas_call x1, Pallas kernels: 27.4 us -> 24.3 us  [per_device(): pl.pallas_call(kernel, name='butterfly', out_shape=jax.ShapeDtypeStruct(b...]
where the time goes in v2:
time: 26.3 us; the launch traced here: 26.2 us
  Pallas kernels  24.3 us (92%)
  local copies, waits for them, and re-layouts  1.89 us (7%)
    pallas_call x1, Pallas kernels, per_device(): pl.pallas_call(kernel, name='butterfly', out_shape=jax.ShapeDtypeStruct(b...  24.3 us
    unnamed x1, local copies, waits for them, and re-layouts  1.89 us

profile of v2, /device:TPU:0, one launch (start us, length us, event | category | flops | bytes accessed | tf_op | source)
XLA Modules:
  0.0 26.2 jit_solution(3557572086569275021)
XLA Ops:
  0.0 24.3 %butterfly.1 = f32[2,8,64,128]{3,2,1,0:T(8,128)} custom-call(s32[64]{0:T(128)} %space_hbm.1, s32[64]{0:T(128)} %wave_hbm.1, f32[2,8,64,128]{3,2,1,0:T(8,128)} %coef_hbm.1, bf16[4,2,128,256]{3,2,1,0:T(8,128)(2,1)} %constant.4.clone.pre_hbm, bf16[4,128,512]{2,1,0:T(8,128)(2,1)} %constant.5.clone.last_hbm), custom_call_target="tpu_custom_call" | custom-call | tf_op jit(solution)/shard_map/butterfly/pallas_call | solution.py:413
  24.3 1.9 %copy.7 = f32[2,8,64,128]{3,2,1,0:T(8,128)} copy(f32[2,8,64,128]{3,2,1,0:T(8,128)} %butterfly.1) | data formatting | bytes 1048576

commit v3 on v2

--- a/solution.py
+++ b/solution.py
@@ -17,7 +17,7 @@
 AHEAD = 3
 LAG_C = 2
 LAG_E = 4
-UNROLL = 8
+UNROLL = 16
 
 NODES = 0.5 - 0.5 * np.cos(np.pi * (2.0 * np.arange(8) + 1.0) / 16.0)
 
@@ -410,6 +410,7 @@
     tile = (8, LANES)
     table = (rank, LANES)
     dma = pltpu.SemaphoreType.DMA
+    operands = [spatial_root, frequency_root, coefficients, jnp.asarray(PRE_TABLE), jnp.asarray(LAST_TABLE)]
     return pl.pallas_call(
         kernel,
         name="butterfly",
@@ -449,9 +450,9 @@
             dma((3, rhs // 2)),
         ],
         compiler_params=pltpu.CompilerParams(
-            collective_id=0, has_side_effects=True, vmem_limit_bytes=60 * 2**20
+            collective_id=0, has_side_effects=True, vmem_limit_bytes=32 * 2**20
         ),
-    )(spatial_root, frequency_root, coefficients, jnp.asarray(PRE_TABLE), jnp.asarray(LAST_TABLE))
+    )(*[pltpu.with_memory_space_constraint(x, pltpu.HBM) for x in operands])
 
 
 def solution(mesh):

time: 26.3 us -> 24.3 us (0.924)
  local copies, waits for them, and re-layouts: 1.89 us -> 0.8 us
  Pallas kernels: 24.3 us -> 23.4 us
    unnamed x1, local copies, waits for them, and re-layouts: 1.89 us -> 0.8 us
    pallas_call x1, Pallas kernels: 24.3 us -> 23.4 us  [per_device(): pl.pallas_call(kernel, name='butterfly', out_shape=jax.ShapeDtypeStruct(b...]
where the time goes in v3:
time: 24.3 us; the launch traced here: 24.2 us
  Pallas kernels  23.4 us (96%)
  local copies, waits for them, and re-layouts  0.8 us (3%)
    pallas_call x1, Pallas kernels, per_device(): pl.pallas_call(kernel, name='butterfly', out_shape=jax.ShapeDtypeStruct(b...  23.4 us
    unnamed x1, local copies, waits for them, and re-layouts  0.8 us

profile of v3, /device:TPU:0, one launch (start us, length us, event | category | flops | bytes accessed | tf_op | source)
XLA Modules:
  0.0 24.2 jit_solution(10844809958614238221)
XLA Ops:
  0.0 23.4 %butterfly.1 = f32[2,8,64,128]{3,2,1,0:T(8,128)S(1)} custom-call(s32[64]{0:T(128)} %space_hbm.1, s32[64]{0:T(128)} %wave_hbm.1, f32[2,8,64,128]{3,2,1,0:T(8,128)} %coef_hbm.1, bf16[4,2,128,256]{3,2,1,0:T(8,128)(2,1)} %constant.4.clone.pre_hbm, bf16[4,128,512]{2,1,0:T(8,128)(2,1)} %constant.5.clone.last_hbm), custom_call_target="tpu_custom_call" | custom-call | tf_op jit(solution)/shard_map/butterfly/pallas_call | solution.py:414
  23.4 0.8 %copy.7 = f32[2,8,64,128]{3,2,1,0:T(8,128)} copy(f32[2,8,64,128]{3,2,1,0:T(8,128)S(1)} %butterfly.1) | data formatting | bytes 1048576
